TPU v7x, 32 devices: a whole 2x2x4 slice. The times are simulated.
32 devices in a mesh: seq: 8 (over z, core), chan: 4 (over y, x).
Axes of the slice: x: 2, y: 2, z: 4, core: 2. Of those that a mesh axis runs over, the one named last changes fastest.
Arguments:
- hidden: bfloat16 [4096, 2560], P('seq'), may hold values from -16 to 16
- embedding: bfloat16 [4096, 2560], P('seq'), may hold values from -16 to 16
- segments: int32 [4096], replicated, may hold values from 0 to 2, never falling along the last dimension, each value on 1 to 3072 neighbouring positions
- input_norm_gain: float32 [2560], replicated, may hold values from 0.5 to 1.5
- gate_proj: bfloat16 [2560, 5120], P(None, 'chan'), may hold values from -0.125 to 0.125
- input_proj: bfloat16 [2560, 5120], P(None, 'chan'), may hold values from -0.125 to 0.125
- state_proj: bfloat16 [2560, 128], replicated, may hold values from -0.125 to 0.125
- step_proj: bfloat16 [2560, 80], P(None, 'chan'), may hold values from -1 to 1
- step_bias: float32 [80], P('chan'), may hold values from -5 to -3
- decay_log: float32 [80], P('chan'), may hold values from -8 to 1
- skip_gain: float32 [80], P('chan'), may hold values from 0.5 to 1.5
- out_gain: float32 [5120], P('chan'), may hold values from 0.5 to 1.5
- out_proj: bfloat16 [5120, 2560], P('chan'), may hold values from -0.078125 to 0.078125
- attn_gain: float32 [5120], replicated, may hold values from 0.5 to 1.5
- query_proj: bfloat16 [5120, 5120], P('seq', 'chan'), may hold values from -1 to 1
- key_proj: bfloat16 [5120, 5120], P('seq', 'chan'), may hold values from -1 to 1
- value_proj: bfloat16 [5120, 5120], P('seq', 'chan'), may hold values from -0.078125 to 0.078125
- attn_out: bfloat16 [5120, 2560], P('chan', 'seq'), may hold values from -0.078125 to 0.078125
Outputs:
- mixed: bfloat16 [4096, 2560], P('seq', 'chan')
Inputs may be any that keep to these rules, and one draw needn't show every extreme that they name: `segments`: document ids never fall along the sequence, and every document has 1 to 3072 positions.
All inputs are finite; a program needn't handle non-finite values.
Results may differ from a plain program's by a relative error of at most 0.0095.
Values may be sent and summed in bfloat16 or wider, within the bound.
A program may use at most 256 MiB of HBM per device.

v0:
```python
import jax
import jax.numpy as jnp
from jax import lax
from jax.sharding import PartitionSpec as P

N = 64
HEAD_CHANNELS = 64
AP = 160
EPSILON = 1e-05
HIGHEST = lax.Precision.HIGHEST


def carried_in(value, axis, combine, identity):
    count, here = (lax.axis_size(axis), lax.axis_index(axis))
    everything = jax.tree.map(lambda part: lax.all_gather(part, axis), value)
    start = jax.tree.map(
        lambda part, zero: jnp.broadcast_to(jnp.asarray(zero, part.dtype), part.shape),
        value,
        identity,
    )

    def lap(k, before):
        reached = k < here
        new = combine(before, jax.tree.map(lambda part: part[k], everything))
        return jax.tree.map(lambda a, b: jnp.where(reached, a, b), new, before)

    return lax.fori_loop(0, count, lap, start)


def normalize(values_in, gain_in):
    widened = values_in.astype(jnp.float32)
    factor = lax.rsqrt(jnp.mean(widened * widened, axis=-1, keepdims=True) + EPSILON)
    return (widened * factor * gain_in).astype(jnp.bfloat16)


def block_terms(inputs_x, steps_dt, rate_vec, b_rows, c_rows, doc_ids, prev_doc):
    block_len = inputs_x.shape[0]
    head_count = steps_dt.shape[1]
    per_head = inputs_x.shape[1] // head_count
    logdecay = steps_dt * rate_vec[None, :]
    running = jnp.cumsum(logdecay, axis=0)
    places = jnp.arange(block_len)
    allowed = (places[:, None] >= places[None, :]) & (doc_ids[:, None] == doc_ids[None, :])
    spread = running.T[:, :, None] - running.T[:, None, :]
    decays = jnp.exp(jnp.where(allowed[None], spread, -1e30))
    intersection = jnp.dot(c_rows, b_rows.T, precision=HIGHEST)
    scaled_x = inputs_x.reshape(block_len, head_count, per_head) * steps_dt[:, :, None]
    intra_out = jnp.einsum("hts,shp->thp", decays * intersection[None], scaled_x, precision=HIGHEST)
    final_doc = doc_ids[block_len - 1]
    keeping = (
        jnp.exp(running[block_len - 1][None, :] - running)
        * (doc_ids == final_doc).astype(jnp.float32)[:, None]
    )
    own_state = jnp.einsum("sn,shp->hnp", b_rows, scaled_x * keeping[:, :, None], precision=HIGHEST)
    through = jnp.exp(running[block_len - 1]) * (final_doc == prev_doc).astype(jnp.float32)
    entering = jnp.exp(running) * (doc_ids == prev_doc).astype(jnp.float32)[:, None]
    return (intra_out, own_state, through, entering)


def carried(c_rows, entering, state_in):
    return jnp.einsum("tn,hnp->thp", c_rows, state_in, precision=HIGHEST) * entering[:, :, None]


def compose(earlier, later):
    return (earlier[0] * later[0], later[0][:, None, None] * earlier[1] + later[1])


def local(
    hidden,
    embedding,
    segments,
    input_norm_gain,
    gate_proj,
    input_proj,
    state_proj,
    step_proj,
    step_bias,
    decay_log,
    skip_gain,
    out_gain,
    out_proj,
    attn_gain,
    query_proj,
    key_proj,
    value_proj,
    attn_out,
):
    tok_rows = hidden.shape[0]
    seq_index = lax.axis_index("seq")
    chan_index = lax.axis_index("chan")
    channel_count = lax.axis_size("chan")
    row_start = seq_index * tok_rows
    tokens_n = normalize(hidden, input_norm_gain)
    gate_z = jnp.dot(tokens_n, gate_proj, preferred_element_type=jnp.float32)
    inputs_x = jax.nn.silu(jnp.dot(tokens_n, input_proj, preferred_element_type=jnp.float32))
    b_and_c = jax.nn.silu(jnp.dot(tokens_n, state_proj, preferred_element_type=jnp.float32))
    b_rows = b_and_c[:, :N]
    c_rows = b_and_c[:, N:]
    steps_dt = jax.nn.softplus(
        jnp.dot(tokens_n, step_proj, preferred_element_type=jnp.float32) + step_bias[None, :]
    )
    rate_vec = -jnp.exp(decay_log)
    doc_ids = lax.dynamic_slice_in_dim(segments, row_start, tok_rows)
    before = lax.dynamic_slice_in_dim(segments, jnp.maximum(row_start - 1, 0), 1)[0]
    prev_doc = jnp.where(seq_index > 0, before, -1)
    intra_out, own_state, through, entering = block_terms(
        inputs_x, steps_dt, rate_vec, b_rows, c_rows, doc_ids, prev_doc
    )
    neutral = (jnp.ones_like(through), jnp.zeros_like(own_state))
    state_in = carried_in((through, own_state), "seq", compose, neutral)[1]
    mixed_y = intra_out + carried(c_rows, entering, state_in)
    y_full = (
        mixed_y.reshape(tok_rows, -1) + inputs_x * jnp.repeat(skip_gain, HEAD_CHANNELS)[None, :]
    )
    gated = y_full * jax.nn.silu(gate_z)
    squares = jnp.sum(gated * gated, axis=-1)
    weighted = (gated * out_gain[None, :]).astype(jnp.bfloat16)
    partial_value = jnp.dot(weighted, out_proj, preferred_element_type=jnp.float32)
    inner_total = gate_proj.shape[1] * channel_count
    feat_width = hidden.shape[1] // channel_count
    shares = lax.psum_scatter(partial_value, "chan", scatter_dimension=1, tiled=True)
    square_total = lax.psum(squares, "chan")
    own_cols = lax.dynamic_slice_in_dim(hidden, chan_index * feat_width, feat_width, 1)
    mixed_share = (
        own_cols.astype(jnp.float32)
        + shares * lax.rsqrt(square_total / inner_total + EPSILON)[:, None]
    ).astype(jnp.bfloat16)
    mixed_h = lax.all_gather(mixed_share, "chan", axis=1, tiled=True)
    joined = jnp.concatenate((mixed_h, embedding), axis=1)
    attention_input = normalize(joined, attn_gain)
    head_cols = query_proj.shape[1]
    pieces = (
        lax.all_gather(query_proj, "seq", axis=0, tiled=True),
        lax.all_gather(key_proj, "seq", axis=0, tiled=True),
        lax.all_gather(value_proj, "seq", axis=0, tiled=True),
    )
    query_sum, key_sum, value_sum = tuple(
        (
            jnp.dot(attention_input, piece_one, preferred_element_type=jnp.float32)
            for piece_one in pieces
        )
    )
    queries = query_sum.astype(jnp.bfloat16)
    keys_all = key_sum.astype(jnp.bfloat16)
    values_all = value_sum.astype(jnp.bfloat16)
    local_heads = head_cols // AP
    query_heads = queries.reshape(tok_rows, local_heads, AP)
    query_places = row_start + jnp.arange(tok_rows)
    scaling = AP ** (-0.5)
    row_max = jnp.full((tok_rows, local_heads), -1e30, jnp.float32)
    key_piece = lax.all_gather(keys_all, "seq", axis=0, tiled=True)
    value_piece = lax.all_gather(values_all, "seq", axis=0, tiled=True)
    piece_rows = key_piece.shape[0]
    key_heads = key_piece.reshape(piece_rows, local_heads, AP)
    value_heads = value_piece.reshape(piece_rows, local_heads, AP)
    scores = (
        jnp.einsum("qhd,khd->qhk", query_heads, key_heads, preferred_element_type=jnp.float32)
        * scaling
    )
    key_places = jnp.arange(piece_rows)
    visible = (key_places[None, :] <= query_places[:, None]) & (
        segments[None, :] == doc_ids[:, None]
    )
    scores = jnp.where(visible[:, None, :], scores, -1e30)
    new_max = jnp.maximum(row_max, jnp.max(scores, axis=-1))
    weights = jnp.exp(scores - new_max[:, :, None])
    row_sum = jnp.sum(weights, axis=-1)
    accum = jnp.einsum(
        "qhk,khd->qhd",
        weights.astype(jnp.bfloat16),
        value_heads,
        preferred_element_type=jnp.float32,
    )
    context = (accum / row_sum[:, :, None]).reshape(tok_rows, head_cols).astype(jnp.bfloat16)
    out_full = jnp.dot(
        context,
        lax.all_gather(attn_out, "seq", axis=1, tiled=True),
        preferred_element_type=jnp.float32,
    )
    out_share = lax.psum_scatter(out_full, "chan", scatter_dimension=1, tiled=True)
    own_mixed = lax.dynamic_slice_in_dim(mixed_h, chan_index * feat_width, feat_width, 1)
    return (out_share + own_mixed.astype(jnp.float32)).astype(jnp.bfloat16)


def solution(mesh):
    in_specs = (
        P("seq", None),
        P("seq", None),
        P(),
        P(),
        P(None, "chan"),
        P(None, "chan"),
        P(),
        P(None, "chan"),
        P("chan"),
        P("chan"),
        P("chan"),
        P("chan"),
        P("chan", None),
        P(),
        P("seq", "chan"),
        P("seq", "chan"),
        P("seq", "chan"),
        P("chan", "seq"),
    )
    out_specs = P("seq", "chan")
    return jax.shard_map(local, mesh=mesh, in_specs=in_specs, out_specs=out_specs, check_vma=False)
```

profile of v0, /device:TPU:0, one launch (start us, length us, event | category | flops | bytes accessed | tf_op | source)
XLA Modules:
  0.0 995.4 jit_solution(13010387898185928960)
XLA Ops:
  14.3 3.3 fusion.51
  19.7 8.4 divide_multiply_fusion
  30.3 2.9 divide_multiply_fusion.1
  40.0 13.5 %all-gather.1 = f32[8,1,20]{2,1,0:T(1,128)S(1)} all-gather(f32[1,1,20]{2,1,0:T(1,128)} %bitcast.98), channel_id=1, replica_groups=mesh['seq'=8,'chan'=4] {'seq'}, dimensions={0}, use_global_device_ids=true | all-gather | bytes 720 | tf_op jit(solution)/shard_map/all_gather | solution.py:15
  56.5 40.8 %all-gather.25.cloned.1.call-done = f32[160,64,64]{2,1,0:T(8,128)} async-done(((f32[20,64,64]{2,1,0:T(8,128)}), f32[160,64,64]{2,1,0:T(8,128)}) %all-gather.25.cloned.1.call-update) | async-done | bytes 2621456 | tf_op jit(solution)/shard_map/all_gather | solution.py:15
  97.4 10.3 %while.14 = (s32[]{:T(128)}, f32[20,64,64]{2,1,0:T(8,128)S(1)}, s32[]{:T(128)}, f32[8,20]{1,0:T(8,128)S(1)}, f32[8,20,64,64]{3,2,1,0:T(8,128)}, /*index=5*/s32[]{:T(128)}, s32[]{:T(128)}) while((s32[]{:T(128)}, f32[20,64,64]{2,1,0:T(8,128)S(1)}, s32[]{:T(128)}, f32[8,20]{1,0:T(8,128)S(1)}, f32[8,20,64,64]{3,2,1,0:T(8,128)}, ...), condition=%wide.region_4.5_spmd.clone, body=%wide.region_3.4_spmd.clone.sunk | while | flops 327684 | bytes 983385 | solution.py:27
  108.8 3.3 fusion.48
  112.1 25.5 %bitcast_add_fusion.1 = f32[512,20,64]{0,2,1:T(8,128)} fusion(f32[512,20,64]{0,2,1:T(8,128)S(1)} %bitcast.89, f32[512,512]{1,0:T(8,128)} %fusion.46, f32[20,512]{1,0:T(8,128)} %bitcast.93, pred[512,512]{1,0:T(8,128)(4,1)} %fusion.43, f32[512,20,64]{0,2,1:T(8,128)S(1)} %bitcast.87, f32[512,20]{0,1:T(8,128)} %get-tuple-element.147, f32[512,20]{0,1:T(8,128)} %copy-done.6), kind=kOutput, calls=%fused_computation.38 | convolution fusion | flops 4044226560 | bytes 9297920 | tf_op jit(solution)/shard_map/hts,shp->thp/dot_general | solution.py:48
  137.6 3.4 copy.57
  141.0 8.7 multiply_reduce_fusion
  149.7 8.2 fusion.35
  158.0 9.9 psum.7
  167.9 50.3 %reduce-scatter.3.cloned.1.call-done = f32[512,640]{1,0:T(8,128)} async-done(((f32[512,2560]{1,0:T(8,128)}), f32[512,640]{1,0:T(8,128)}) %reduce-scatter.3.cloned.1.call-update) | async-done | bytes 1310736 | tf_op jit(solution)/shard_map/reduce_scatter | solution.py:121
  222.3 37.9 %all-gather.11.cloned.1.call-done = bf16[512,2560]{1,0:T(8,128)(2,1)} async-done(((bf16[512,640]{1,0:T(8,128)(2,1)}), bf16[512,2560]{1,0:T(8,128)(2,1)}) %all-gather.11.cloned.1.call-update) | async-done | bytes 2621456 | tf_op jit(solution)/shard_map/all_gather | solution.py:128
  260.2 3.8 fusion.12
  264.0 118.7 %all-gather.17.cloned.1.call-done = bf16[5120,1280]{1,0:T(8,128)(2,1)} async-done(((bf16[640,1280]{1,0:T(8,128)(2,1)}), bf16[5120,1280]{1,0:T(8,128)(2,1)}) %all-gather.17.cloned.1.call-update) | async-done | bytes 13107216 | tf_op jit(solution)/shard_map/all_gather | solution.py:134
  382.8 13.3 %convolution_convert_fusion.1 = bf16[512,1280]{1,0:T(8,128)(2,1)} fusion(bf16[5120,1280]{1,0:T(8,128)(2,1)} %all-gather.17.cloned.1.call-done, f32[5120]{0:T(1024)S(1)} %copy-done.12, f32[512]{0:T(512)S(1)} %add_rsqrt_fusion, bf16[512,2560]{1,0:T(8,128)(2,1)} %param.21, bf16[512,2560]{1,0:T(8,128)(2,1)S(1)} %copy-done.4), kind=kOutput, calls=%fused_computation.34 | convolution fusion | flops 6729891840 | bytes 19683328 | tf_op jit(solution)/shard_map/dot_general | solution.py:139
  396.1 107.4 %all-gather.13.cloned.1.call-done = bf16[5120,1280]{1,0:T(8,128)(2,1)} async-done(((bf16[640,1280]{1,0:T(8,128)(2,1)}), bf16[5120,1280]{1,0:T(8,128)(2,1)}) %all-gather.13.cloned.1.call-update) | async-done | bytes 13107216 | tf_op jit(solution)/shard_map/all_gather | solution.py:135
  503.5 13.2 %convolution_convert_fusion.2 = bf16[512,1280]{1,0:T(8,128)(2,1)} fusion(bf16[5120,1280]{1,0:T(8,128)(2,1)} %all-gather.13.cloned.1.call-done, f32[5120]{0:T(1024)S(1)} %copy-done.12, f32[512]{0:T(512)S(1)} %add_rsqrt_fusion, bf16[512,2560]{1,0:T(8,128)(2,1)} %param.21, bf16[512,2560]{1,0:T(8,128)(2,1)S(1)} %copy-done.4), kind=kOutput, calls=%fused_computation.35 | convolution fusion | flops 6729891840 | bytes 19683328 | tf_op jit(solution)/shard_map/dot_general | solution.py:139
  517.5 2.6 fusion.20
  520.2 104.0 %all-gather.21.cloned.1.call-done = bf16[5120,1280]{1,0:T(8,128)(2,1)} async-done(((bf16[640,1280]{1,0:T(8,128)(2,1)}), bf16[5120,1280]{1,0:T(8,128)(2,1)}) %all-gather.21.cloned.1.call-update) | async-done | bytes 13107216 | tf_op jit(solution)/shard_map/all_gather | solution.py:133
  624.2 13.6 %convolution_convert_fusion = bf16[512,1280]{1,0:T(8,128)(2,1)} fusion(bf16[5120,1280]{1,0:T(8,128)(2,1)} %all-gather.21.cloned.1.call-done, f32[5120]{0:T(1024)S(1)} %copy-done.12, f32[512]{0:T(512)S(1)} %add_rsqrt_fusion, bf16[512,2560]{1,0:T(8,128)(2,1)} %param.21, bf16[512,2560]{1,0:T(8,128)(2,1)} %all-gather.11.cloned.1.call-done), kind=kOutput, calls=%fused_computation.33 | convolution fusion | flops 6729891840 | bytes 19683328 | tf_op jit(solution)/shard_map/dot_general | solution.py:139
  637.8 2.4 copy.60
  640.3 83.2 %all-gather.19.cloned.1.call-done = bf16[4096,1280]{1,0:T(8,128)(2,1)} async-done(((bf16[512,1280]{1,0:T(8,128)(2,1)}), bf16[4096,1280]{1,0:T(8,128)(2,1)}) %all-gather.19.cloned.1.call-update) | async-done | bytes 10485776 | tf_op jit(solution)/shard_map/all_gather | solution.py:151
  723.4 14.5 %copy.59 = bf16[4096,1280]{0,1:T(8,128)(2,1)} copy(bf16[4096,1280]{1,0:T(8,128)(2,1)} %all-gather.19.cloned.1.call-done) | data formatting | bytes 20971520 | tf_op jit(solution)/shard_map/all_gather | solution.py:151
  737.9 84.9 %all-gather.15.cloned.1.call-done = bf16[4096,1280]{1,0:T(8,128)(2,1)} async-done(((bf16[512,1280]{1,0:T(8,128)(2,1)}), bf16[4096,1280]{1,0:T(8,128)(2,1)}) %all-gather.15.cloned.1.call-update) | async-done | bytes 10485776 | tf_op jit(solution)/shard_map/all_gather | solution.py:152
  822.8 14.5 %copy.58 = bf16[4096,1280]{0,1:T(8,128)(2,1)} copy(bf16[4096,1280]{1,0:T(8,128)(2,1)} %all-gather.15.cloned.1.call-done) | data formatting | bytes 20971520 | tf_op jit(solution)/shard_map/all_gather | solution.py:152
  837.3 28.4 %fusion.3 = (f32[512,8]{0,1:T(8,128)S(1)}, f32[8,4096,512]{2,1,0:T(8,128)}) fusion(pred[512,4096]{0,1:T(8,128)(4,1)S(1)} %fusion.20, bf16[4096,8,160]{0,2,1:T(8,128)(2,1)} %bitcast.85, bf16[512,8,160]{0,2,1:T(8,128)(2,1)} %bitcast.92), kind=kOutput, calls=%fused_computation.7 | convolution fusion | flops 5419036672 | bytes 81018880 | tf_op jit(solution)/shard_map/qhd,khd->qhk/dot_general | solution.py:157
  865.7 22.0 %fusion.1 = f32[512,8]{0,1:T(8,128)S(1)} fusion(f32[8,4096,512]{2,1,0:T(8,128)} %get-tuple-element.156, f32[512,8]{0,1:T(8,128)S(1)} %broadcast_maximum_fusion, pred[512,4096]{0,1:T(8,128)(4,1)S(1)} %fusion.20), kind=kLoop, calls=%fused_computation.5 | loop fusion | flops 67104768 | bytes 69238784 | tf_op jit(solution)/shard_map/reduce_sum | solution.py:167
  887.7 29.2 %fusion.24 = bf16[512,8,160]{0,2,1:T(8,128)(2,1)} fusion(bf16[4096,8,160]{0,2,1:T(8,128)(2,1)} %bitcast.84, f32[8,4096,512]{2,1,0:T(8,128)} %get-tuple-element.156, f32[512,8]{0,1:T(8,128)S(1)} %broadcast_maximum_fusion, pred[512,4096]{0,1:T(8,128)(4,1)S(1)} %fusion.20, f32[512,8]{0,1:T(8,128)S(1)} %fusion.1), kind=kOutput, calls=%fused_computation.37 | convolution fusion | flops 5437128704 | bytes 81035264 | tf_op jit(solution)/shard_map/qhk,khd->qhd/dot_general | solution.py:168
  916.9 9.2 fusion.73
  926.2 59.7 %reduce-scatter.5.cloned.1.call-done = f32[512,640]{1,0:T(8,128)} async-done(((f32[512,2560]{1,0:T(8,128)}), f32[512,640]{1,0:T(8,128)}) %reduce-scatter.5.cloned.1.call-update) | async-done | bytes 1310736 | tf_op jit(solution)/shard_map/reduce_scatter | solution.py:180
  (103 shorter events, 39.0 us)
Async XLA Ops:
  6.5 23.7 %copy-start = (bf16[2560,128]{1,0:T(8,128)(2,1)S(1)}, bf16[2560,128]{1,0:T(8,128)(2,1)}, u32[]{:S(2)}) copy-start(bf16[2560,128]{1,0:T(8,128)(2,1)} %param.26) | copy-start | bytes 1966084
  6.5 13.2 %copy-start.2 = (bf16[512,2560]{1,0:T(8,128)(2,1)S(1)}, bf16[512,2560]{1,0:T(8,128)(2,1)}, u32[]{:S(2)}) copy-start(bf16[512,2560]{1,0:T(8,128)(2,1)} %param.20) | copy-start | bytes 7864324
  6.5 13.2 %copy-start.13 = (f32[2560]{0:T(1024)S(1)}, f32[2560]{0:T(1024)}, u32[]{:S(2)}) copy-start(f32[2560]{0:T(1024)} %param.23) | copy-start | bytes 30724
  6.5 90.8 %all-gather.25.cloned.1.call-start = ((), (), s32[]{:S(2)}) async-start(), calls=%async_computation.11 | async-start | bytes 5898240 | tf_op jit(solution)/shard_map/all_gather | solution.py:15
  13.6 16.6 %copy-start.10 = (f32[512]{0:T(512)}, f32[512]{0:T(512)S(1)}, u32[]{:S(2)}) copy-start(f32[512]{0:T(512)S(1)} %add_rsqrt_fusion.2) | copy-start | bytes 6148
  30.3 2.9 copy-start.5
  30.3 3.7 copy-start.7
  34.6 0.6 copy-start.6
  38.5 179.6 %reduce-scatter.3.cloned.1.call-start = ((), (), s32[]{:S(2)}) async-start(), calls=%async_computation.2 | async-start | bytes 6553600 | tf_op jit(solution)/shard_map/reduce_scatter | solution.py:121
  137.6 3.4 copy-start.3
  137.6 3.4 copy-start.9
  137.6 3.4 copy-start.11
  137.6 3.4 copy-start.14
  141.0 8.7 copy-start.15
  157.9 102.3 %all-gather.11.cloned.1.call-start = ((), (), s32[]{:S(2)}) async-start(), calls=%async_computation.3 | async-start | bytes 3276800 | tf_op jit(solution)/shard_map/all_gather | solution.py:128
  220.5 162.2 %copy-start.12 = (f32[5120]{0:T(1024)S(1)}, f32[5120]{0:T(1024)}, u32[]{:S(2)}) copy-start(f32[5120]{0:T(1024)} %param.33) | copy-start | bytes 61444
  220.5 162.2 %all-gather.17.cloned.1.call-start = ((), (), s32[]{:S(2)}) async-start(), calls=%async_computation.6 | async-start | bytes 14745600 | tf_op jit(solution)/shard_map/all_gather | solution.py:134
  221.1 282.3 %all-gather.13.cloned.1.call-start = ((), (), s32[]{:S(2)}) async-start(), calls=%async_computation.4 | async-start | bytes 14745600 | tf_op jit(solution)/shard_map/all_gather | solution.py:135
  221.7 402.5 %all-gather.21.cloned.1.call-start = ((), (), s32[]{:S(2)}) async-start(), calls=%async_computation.8 | async-start | bytes 14745600 | tf_op jit(solution)/shard_map/all_gather | solution.py:133
  222.3 501.1 %all-gather.19.cloned.1.call-start = ((), (), s32[]{:S(2)}) async-start(), calls=%async_computation.7 | async-start | bytes 11796480 | tf_op jit(solution)/shard_map/all_gather | solution.py:151
  260.2 122.5 %copy-start.4 = (bf16[512,2560]{1,0:T(8,128)(2,1)S(1)}, bf16[512,2560]{1,0:T(8,128)(2,1)}, u32[]{:S(2)}) copy-start(bf16[512,2560]{1,0:T(8,128)(2,1)} %all-gather.11.cloned.1.call-done) | copy-start | bytes 7864324
  396.1 121.5 %copy-start.8 = (s32[4096]{0:T(1024)S(1)}, s32[4096]{0:T(1024)}, u32[]{:S(2)}) copy-start(s32[4096]{0:T(1024)} %param.22) | copy-start | bytes 49156
  396.1 426.7 %all-gather.15.cloned.1.call-start = ((), (), s32[]{:S(2)}) async-start(), calls=%async_computation.5 | async-start | bytes 11796480 | tf_op jit(solution)/shard_map/all_gather | solution.py:152
  516.7 400.2 %all-gather.23.cloned.1.call-start = ((), (), s32[]{:S(2)}) async-start(), calls=%async_computation.9 | async-start | bytes 7372800 | tf_op jit(solution)/shard_map/all_gather | solution.py:177
  517.5 468.5 %reduce-scatter.5.cloned.1.call-start = ((), (), s32[]{:S(2)}) async-start(), calls=%async_computation.10 | async-start | bytes 6553600 | tf_op jit(solution)/shard_map/reduce_scatter | solution.py:180
  916.9 71.4 %copy-start.1 = (bf16[2560,128]{1,0:T(8,128)(2,1)S(1)}, bf16[2560,128]{1,0:T(8,128)(2,1)}, u32[]{:S(2)}) copy-start(bf16[2560,128]{1,0:T(8,128)(2,1)} %param.26) | copy-start | bytes 1966084
Sparse Core Ops, SparseCore 0:
  38.6 58.6 all-gather.24
  158.0 60.0 reduce-scatter.2
  220.7 39.5 all-gather.10
  261.7 120.9 all-gather.16
  384.3 119.1 all-gather.12
  505.0 119.1 all-gather.20
  625.8 97.5 all-gather.18
  725.1 97.6 all-gather.14
  824.5 65.1 all-gather.22
  926.3 59.5 reduce-scatter.4
where the time goes:
time: 1000 us; the launch traced here: 995 us
  waiting for transfers between devices  689 us (69%)
  matrix products  171 us (17%)
  other arithmetic  51.1 us (5%)
  local copies, waits for them, and re-layouts  44.1 us (4%)
  blocking collectives  23.4 us (2%)
  between operations  15.3 us (2%)
    all_gather x1, waiting for transfers between devices, local(): lax.all_gather(key_proj, 'seq', axis=0, tiled=True)  119 us
    all_gather x1, waiting for transfers between devices, local(): lax.all_gather(value_proj, 'seq', axis=0, tiled=True)  107 us
    all_gather x1, waiting for transfers between devices, local(): lax.all_gather(query_proj, 'seq', axis=0, tiled=True)  104 us
    all_gather x1, waiting for transfers between devices, local(): value_piece = lax.all_gather(values_all, 'seq', axis=0, tiled=True)  84.9 us
    all_gather x1, waiting for transfers between devices, local(): key_piece = lax.all_gather(keys_all, 'seq', axis=0, tiled=True)  83.2 us
    reduce_scatter x1, waiting for transfers between devices, local(): lax.psum_scatter(out_full, 'chan', scatter_dimension=1, tiled=True)  59.7 us
    reduce_scatter x1, waiting for transfers between devices, local(): lax.psum_scatter(partial_value, 'chan', scatter_dimension=1, tiled=True)  50.3 us
    all_gather x1, waiting for transfers between devices, carried_in(): everything = jax.tree.map(lambda part: lax.all_gather(part, axis), value)  40.8 us
  transfers between devices with their start and end apart: 10, of which 9 were waited for; matrix products, arithmetic and copies ran while one was open for 16% of the time, Pallas kernels for 0%

commit v1 on v0

--- a/solution.py
+++ b/solution.py
@@ -8,6 +8,13 @@
 AP = 160
 EPSILON = 1e-05
 HIGHEST = lax.Precision.HIGHEST
+
+
+def bind_signs(field, sheet):
+    piece_now = lax.all_gather(
+        jnp.concatenate([field, sheet], 1), axis_name="seq", axis=0, tiled=True
+    )
+    return jnp.split(piece_now, [field.shape[1]], 1)
 
 
 def carried_in(value, axis, combine, identity):
@@ -148,8 +155,7 @@
     query_places = row_start + jnp.arange(tok_rows)
     scaling = AP ** (-0.5)
     row_max = jnp.full((tok_rows, local_heads), -1e30, jnp.float32)
-    key_piece = lax.all_gather(keys_all, "seq", axis=0, tiled=True)
-    value_piece = lax.all_gather(values_all, "seq", axis=0, tiled=True)
+    key_piece, value_piece = bind_signs(keys_all, sheet=values_all)
     piece_rows = key_piece.shape[0]
     key_heads = key_piece.reshape(piece_rows, local_heads, AP)
     value_heads = value_piece.reshape(piece_rows, local_heads, AP)

time: 1000 us -> 1020 us (1.020)
  local copies, waits for them, and re-layouts: 44.1 us -> 59.9 us
    split x0 -> x3, local copies, waits for them, and re-layouts: none -> 44.8 us  [bind_signs(): return jnp.split(piece_now, [field.shape[1]], 1)]
    all_gather x2 -> x0, local copies, waits for them, and re-layouts: 29 us -> none  [the longest x1 14.5 us: local(): value_piece = lax.all_gather(values_all, 'seq', axis=0, tiled=True)]
    all_gather x1, waiting for transfers between devices: 107 us -> 119 us  [local(): lax.all_gather(value_proj, 'seq', axis=0, tiled=True)]
    all_gather x1, waiting for transfers between devices: 119 us -> 107 us  [local(): lax.all_gather(key_proj, 'seq', axis=0, tiled=True)]
    all_gather x2 -> x1, waiting for transfers between devices: 168 us -> 169 us  [bind_signs(): lax.all_gather(jnp.concatenate([field, sheet], 1), axis_name='seq', axis=...]
  transfers between devices with their start and end apart: 10 -> 9, of which waited for: 9 -> 8; matrix products, arithmetic and copies ran while one was open for 16% -> 18% of each run, Pallas kernels for 0% -> 0%
where the time goes in v1:
time: 1020 us; the launch traced here: 1010 us
  waiting for transfers between devices  689 us (68%)
  matrix products  170 us (17%)
  local copies, waits for them, and re-layouts  59.9 us (6%)
  other arithmetic  52.3 us (5%)
  blocking collectives  23.6 us (2%)
  between operations  15 us (1%)
    all_gather x1, waiting for transfers between devices, bind_signs(): lax.all_gather(jnp.concatenate([field, sheet], 1), axis_name='seq', axis=...  169 us
    all_gather x1, waiting for transfers between devices, local(): lax.all_gather(value_proj, 'seq', axis=0, tiled=True)  119 us
    all_gather x1, waiting for transfers between devices, local(): lax.all_gather(key_proj, 'seq', axis=0, tiled=True)  107 us
    all_gather x1, waiting for transfers between devices, local(): lax.all_gather(query_proj, 'seq', axis=0, tiled=True)  103 us
    reduce_scatter x1, waiting for transfers between devices, local(): lax.psum_scatter(out_full, 'chan', scatter_dimension=1, tiled=True)  59.6 us
    reduce_scatter x1, waiting for transfers between devices, local(): lax.psum_scatter(partial_value, 'chan', scatter_dimension=1, tiled=True)  50.2 us
    split x3, local copies, waits for them, and re-layouts, bind_signs(): return jnp.split(piece_now, [field.shape[1]], 1)  44.8 us
    all_gather x1, waiting for transfers between devices, carried_in(): everything = jax.tree.map(lambda part: lax.all_gather(part, axis), value)  40.7 us
  transfers between devices with their start and end apart: 9, of which 8 were waited for; matrix products, arithmetic and copies ran while one was open for 18% of the time, Pallas kernels for 0%

profile of v1, /device:TPU:0, one launch (start us, length us, event | category | flops | bytes accessed | tf_op | source)
XLA Modules:
  0.0 1011.2 jit_solution(18077290942200927381)
XLA Ops:
  14.3 3.3 fusion.51
  19.7 8.4 divide_multiply_fusion
  30.3 2.9 divide_multiply_fusion.1
  40.0 13.7 %all-gather.1 = f32[8,1,20]{2,1,0:T(1,128)S(1)} all-gather(f32[1,1,20]{2,1,0:T(1,128)} %bitcast.98), channel_id=1, replica_groups=mesh['seq'=8,'chan'=4] {'seq'}, dimensions={0}, use_global_device_ids=true | all-gather | bytes 720 | tf_op jit(solution)/shard_map/all_gather | solution.py:22
  56.7 40.7 %all-gather.22.cloned.1.call-done = f32[160,64,64]{2,1,0:T(8,128)} async-done(((f32[20,64,64]{2,1,0:T(8,128)}), f32[160,64,64]{2,1,0:T(8,128)}) %all-gather.22.cloned.1.call-update) | async-done | bytes 2621456 | tf_op jit(solution)/shard_map/all_gather | solution.py:22
  97.4 10.3 %while.14 = (s32[]{:T(128)}, f32[20,64,64]{2,1,0:T(8,128)S(1)}, s32[]{:T(128)}, f32[8,20]{1,0:T(8,128)S(1)}, f32[8,20,64,64]{3,2,1,0:T(8,128)}, /*index=5*/s32[]{:T(128)}, s32[]{:T(128)}) while((s32[]{:T(128)}, f32[20,64,64]{2,1,0:T(8,128)S(1)}, s32[]{:T(128)}, f32[8,20]{1,0:T(8,128)S(1)}, f32[8,20,64,64]{3,2,1,0:T(8,128)}, ...), condition=%wide.region_4.5_spmd.clone, body=%wide.region_3.4_spmd.clone.sunk | while | flops 327684 | bytes 983393 | solution.py:34
  108.8 3.3 fusion.48
  112.1 25.5 %bitcast_add_fusion.1 = f32[512,20,64]{0,2,1:T(8,128)} fusion(f32[512,20,64]{0,2,1:T(8,128)S(1)} %bitcast.89, f32[512,512]{1,0:T(8,128)} %fusion.46, f32[20,512]{1,0:T(8,128)} %bitcast.93, pred[512,512]{1,0:T(8,128)(4,1)} %fusion.43, f32[512,20,64]{0,2,1:T(8,128)S(1)} %bitcast.87, f32[512,20]{0,1:T(8,128)} %get-tuple-element.149, f32[512,20]{0,1:T(8,128)} %copy-done.7), kind=kOutput, calls=%fused_computation.39 | convolution fusion | flops 4044226560 | bytes 9297920 | tf_op jit(solution)/shard_map/hts,shp->thp/dot_general | solution.py:55
  137.6 3.4 copy.57
  141.0 8.7 multiply_reduce_fusion
  149.7 8.2 fusion.35
  158.0 9.9 psum.7
  167.9 50.2 %reduce-scatter.3.cloned.1.call-done = f32[512,640]{1,0:T(8,128)} async-done(((f32[512,2560]{1,0:T(8,128)}), f32[512,640]{1,0:T(8,128)}) %reduce-scatter.3.cloned.1.call-update) | async-done | bytes 1310736 | tf_op jit(solution)/shard_map/reduce_scatter | solution.py:128
  222.4 37.9 %all-gather.10.cloned.1.call-done = bf16[512,2560]{1,0:T(8,128)(2,1)} async-done(((bf16[512,640]{1,0:T(8,128)(2,1)}), bf16[512,2560]{1,0:T(8,128)(2,1)}) %all-gather.10.cloned.1.call-update) | async-done | bytes 2621456 | tf_op jit(solution)/shard_map/all_gather | solution.py:135
  260.2 3.8 fusion.12
  264.0 118.7 %all-gather.14.cloned.1.call-done = bf16[5120,1280]{1,0:T(8,128)(2,1)} async-done(((bf16[640,1280]{1,0:T(8,128)(2,1)}), bf16[5120,1280]{1,0:T(8,128)(2,1)}) %all-gather.14.cloned.1.call-update) | async-done | bytes 13107216 | tf_op jit(solution)/shard_map/all_gather | solution.py:142
  382.8 13.2 %convolution_convert_fusion.1 = bf16[512,1280]{1,0:T(8,128)(2,1)} fusion(bf16[5120,1280]{1,0:T(8,128)(2,1)} %all-gather.14.cloned.1.call-done, f32[5120]{0:T(1024)S(1)} %copy-done.13, f32[512]{0:T(512)S(1)} %add_rsqrt_fusion, bf16[512,2560]{1,0:T(8,128)(2,1)} %param.21, bf16[512,2560]{1,0:T(8,128)(2,1)S(1)} %copy-done.4), kind=kOutput, calls=%fused_computation.34 | convolution fusion | flops 6729891840 | bytes 19683328 | tf_op jit(solution)/shard_map/dot_general | solution.py:146
  396.0 107.5 %all-gather.12.cloned.1.call-done = bf16[5120,1280]{1,0:T(8,128)(2,1)} async-done(((bf16[640,1280]{1,0:T(8,128)(2,1)}), bf16[5120,1280]{1,0:T(8,128)(2,1)}) %all-gather.12.cloned.1.call-update) | async-done | bytes 13107216 | tf_op jit(solution)/shard_map/all_gather | solution.py:141
  503.5 12.5 %convolution_convert_fusion.2 = bf16[512,1280]{1,0:T(8,128)(2,1)S(1)} fusion(bf16[5120,1280]{1,0:T(8,128)(2,1)} %all-gather.12.cloned.1.call-done, f32[5120]{0:T(1024)S(1)} %copy-done.13, f32[512]{0:T(512)S(1)} %add_rsqrt_fusion, bf16[512,2560]{1,0:T(8,128)(2,1)} %param.21, bf16[512,2560]{1,0:T(8,128)(2,1)S(1)} %copy-done.4), kind=kOutput, calls=%fused_computation.35 | convolution fusion | flops 6729891840 | bytes 19683328 | tf_op jit(solution)/shard_map/dot_general | solution.py:146
  518.5 2.6 fusion.20
  521.1 103.1 %all-gather.18.cloned.1.call-done = bf16[5120,1280]{1,0:T(8,128)(2,1)} async-done(((bf16[640,1280]{1,0:T(8,128)(2,1)}), bf16[5120,1280]{1,0:T(8,128)(2,1)}) %all-gather.18.cloned.1.call-update) | async-done | bytes 13107216 | tf_op jit(solution)/shard_map/all_gather | solution.py:140
  624.2 13.6 %convolution_convert_fusion = bf16[512,1280]{1,0:T(8,128)(2,1)} fusion(bf16[5120,1280]{1,0:T(8,128)(2,1)} %all-gather.18.cloned.1.call-done, f32[5120]{0:T(1024)S(1)} %copy-done.13, f32[512]{0:T(512)S(1)} %add_rsqrt_fusion, bf16[512,2560]{1,0:T(8,128)(2,1)} %param.21, bf16[512,2560]{1,0:T(8,128)(2,1)} %all-gather.10.cloned.1.call-done), kind=kOutput, calls=%fused_computation.33 | convolution fusion | flops 6729891840 | bytes 19683328 | tf_op jit(solution)/shard_map/dot_general | solution.py:146
  637.9 2.5 copy.60
  640.3 169.2 %all-gather.16.cloned.1.call-done = bf16[4096,2560]{1,0:T(8,128)(2,1)} async-done(((bf16[512,2560]{1,0:T(8,128)(2,1)}), bf16[4096,2560]{1,0:T(8,128)(2,1)}) %all-gather.16.cloned.1.call-update) | async-done | bytes 20971536 | tf_op jit(solution)/shard_map/all_gather | solution.py:14
  809.5 16.1 %fusion.73 = (bf16[4096,1280]{1,0:T(8,128)(2,1)}, bf16[4096,1280]{1,0:T(8,128)(2,1)}) fusion(bf16[4096,2560]{1,0:T(8,128)(2,1)} %all-gather.16.cloned.1.call-done), kind=kLoop, calls=%fused_computation.96 | loop fusion | bytes 41943040 | tf_op jit(solution)/shard_map/split | solution.py:17
  825.6 14.3 %copy.58 = bf16[4096,1280]{0,1:T(8,128)(2,1)} copy(bf16[4096,1280]{1,0:T(8,128)(2,1)} %get-tuple-element.148) | data formatting | bytes 20971520 | tf_op jit(solution)/shard_map/split | solution.py:17
  839.9 14.4 %copy.59 = bf16[4096,1280]{0,1:T(8,128)(2,1)} copy(bf16[4096,1280]{1,0:T(8,128)(2,1)} %get-tuple-element.147) | data formatting | bytes 20971520 | tf_op jit(solution)/shard_map/split | solution.py:17
  854.3 28.1 %fusion.3 = (f32[512,8]{0,1:T(8,128)S(1)}, f32[8,4096,512]{2,1,0:T(8,128)}) fusion(pred[512,4096]{0,1:T(8,128)(4,1)S(1)} %fusion.20, bf16[4096,8,160]{0,2,1:T(8,128)(2,1)} %bitcast.85, bf16[512,8,160]{0,2,1:T(8,128)(2,1)} %bitcast.92), kind=kOutput, calls=%fused_computation.7 | convolution fusion | flops 5419036672 | bytes 81018880 | tf_op jit(solution)/shard_map/qhd,khd->qhk/dot_general | solution.py:163
  882.4 21.5 %fusion.1 = f32[512,8]{0,1:T(8,128)S(1)} fusion(f32[8,4096,512]{2,1,0:T(8,128)} %get-tuple-element.158, f32[512,8]{0,1:T(8,128)S(1)} %broadcast_maximum_fusion, pred[512,4096]{0,1:T(8,128)(4,1)S(1)} %fusion.20), kind=kLoop, calls=%fused_computation.5 | loop fusion | flops 67104768 | bytes 69238784 | tf_op jit(solution)/shard_map/reduce_sum | solution.py:173
  903.9 29.2 %fusion.24 = bf16[512,8,160]{0,2,1:T(8,128)(2,1)} fusion(bf16[4096,8,160]{0,2,1:T(8,128)(2,1)} %bitcast.84, f32[8,4096,512]{2,1,0:T(8,128)} %get-tuple-element.158, f32[512,8]{0,1:T(8,128)S(1)} %broadcast_maximum_fusion, pred[512,4096]{0,1:T(8,128)(4,1)S(1)} %fusion.20, f32[512,8]{0,1:T(8,128)S(1)} %fusion.1), kind=kOutput, calls=%fused_computation.38 | convolution fusion | flops 5437128704 | bytes 81035264 | tf_op jit(solution)/shard_map/qhk,khd->qhd/dot_general | solution.py:174
  933.1 9.2 fusion.74
  942.4 59.6 %reduce-scatter.5.cloned.1.call-done = f32[512,640]{1,0:T(8,128)} async-done(((f32[512,2560]{1,0:T(8,128)}), f32[512,640]{1,0:T(8,128)}) %reduce-scatter.5.cloned.1.call-update) | async-done | bytes 1310736 | tf_op jit(solution)/shard_map/reduce_scatter | solution.py:186
  (104 shorter events, 40.6 us)
Async XLA Ops:
  6.5 23.8 %copy-start = (bf16[2560,128]{1,0:T(8,128)(2,1)S(1)}, bf16[2560,128]{1,0:T(8,128)(2,1)}, u32[]{:S(2)}) copy-start(bf16[2560,128]{1,0:T(8,128)(2,1)} %param.26) | copy-start | bytes 1966084
  6.5 13.2 %copy-start.2 = (bf16[512,2560]{1,0:T(8,128)(2,1)S(1)}, bf16[512,2560]{1,0:T(8,128)(2,1)}, u32[]{:S(2)}) copy-start(bf16[512,2560]{1,0:T(8,128)(2,1)} %param.20) | copy-start | bytes 7864324
  6.5 13.2 %copy-start.14 = (f32[2560]{0:T(1024)S(1)}, f32[2560]{0:T(1024)}, u32[]{:S(2)}) copy-start(f32[2560]{0:T(1024)} %param.23) | copy-start | bytes 30724
  6.5 90.8 %all-gather.22.cloned.1.call-start = ((), (), s32[]{:S(2)}) async-start(), calls=%async_computation.10 | async-start | bytes 5898240 | tf_op jit(solution)/shard_map/all_gather | solution.py:22
  13.6 16.6 %copy-start.11 = (f32[512]{0:T(512)}, f32[512]{0:T(512)S(1)}, u32[]{:S(2)}) copy-start(f32[512]{0:T(512)S(1)} %add_rsqrt_fusion.2) | copy-start | bytes 6148
  30.3 2.9 copy-start.6
  30.3 3.6 copy-start.8
  34.6 0.6 copy-start.7
  38.5 179.6 %reduce-scatter.3.cloned.1.call-start = ((), (), s32[]{:S(2)}) async-start(), calls=%async_computation.2 | async-start | bytes 6553600 | tf_op jit(solution)/shard_map/reduce_scatter | solution.py:128
  137.6 3.4 copy-start.3
  137.6 3.4 copy-start.10
  137.6 3.4 copy-start.12
  137.6 3.4 copy-start.15
  141.0 8.7 copy-start.16
  157.9 102.3 %all-gather.10.cloned.1.call-start = ((), (), s32[]{:S(2)}) async-start(), calls=%async_computation.3 | async-start | bytes 3276800 | tf_op jit(solution)/shard_map/all_gather | solution.py:135
  220.5 162.2 %copy-start.13 = (f32[5120]{0:T(1024)S(1)}, f32[5120]{0:T(1024)}, u32[]{:S(2)}) copy-start(f32[5120]{0:T(1024)} %param.33) | copy-start | bytes 61444
  220.6 162.2 %all-gather.14.cloned.1.call-start = ((), (), s32[]{:S(2)}) async-start(), calls=%async_computation.5 | async-start | bytes 14745600 | tf_op jit(solution)/shard_map/all_gather | solution.py:142
  221.1 282.3 %all-gather.12.cloned.1.call-start = ((), (), s32[]{:S(2)}) async-start(), calls=%async_computation.4 | async-start | bytes 14745600 | tf_op jit(solution)/shard_map/all_gather | solution.py:141
  221.7 402.5 %all-gather.18.cloned.1.call-start = ((), (), s32[]{:S(2)}) async-start(), calls=%async_computation.7 | async-start | bytes 14745600 | tf_op jit(solution)/shard_map/all_gather | solution.py:140
  222.3 587.2 %all-gather.16.cloned.1.call-start = ((), (), s32[]{:S(2)}) async-start(), calls=%async_computation.6 | async-start | bytes 23592960 | tf_op jit(solution)/shard_map/all_gather | solution.py:14
  260.2 122.5 %copy-start.4 = (bf16[512,2560]{1,0:T(8,128)(2,1)S(1)}, bf16[512,2560]{1,0:T(8,128)(2,1)}, u32[]{:S(2)}) copy-start(bf16[512,2560]{1,0:T(8,128)(2,1)} %all-gather.10.cloned.1.call-done) | copy-start | bytes 7864324
  503.5 12.5 %copy-start.5 = (bf16[512,1280]{1,0:T(8,128)(2,1)S(1)}, bf16[512,1280]{1,0:T(8,128)(2,1)}, u32[]{:S(2)}) copy-start(bf16[512,1280]{1,0:T(8,128)(2,1)} %convolution_convert_fusion.1) | copy-start | bytes 3932164
  516.0 2.5 copy-start.9
  517.7 415.4 %all-gather.20.cloned.1.call-start = ((), (), s32[]{:S(2)}) async-start(), calls=%async_computation.8 | async-start | bytes 7372800 | tf_op jit(solution)/shard_map/all_gather | solution.py:183
  518.4 483.6 %reduce-scatter.5.cloned.1.call-start = ((), (), s32[]{:S(2)}) async-start(), calls=%async_computation.9 | async-start | bytes 6553600 | tf_op jit(solution)/shard_map/reduce_scatter | solution.py:186
  933.1 71.3 %copy-start.1 = (bf16[2560,128]{1,0:T(8,128)(2,1)S(1)}, bf16[2560,128]{1,0:T(8,128)(2,1)}, u32[]{:S(2)}) copy-start(bf16[2560,128]{1,0:T(8,128)(2,1)} %param.26) | copy-start | bytes 1966084
Sparse Core Ops, SparseCore 0:
  38.6 58.7 all-gather.21
  158.0 60.0 reduce-scatter.2
  220.7 39.5 all-gather.9
  261.7 120.9 all-gather.13
  384.3 119.1 all-gather.11
  505.0 119.1 all-gather.17
  625.8 183.6 all-gather.15
  811.2 65.0 all-gather.19
  942.5 59.4 reduce-scatter.4
